TPU v7x, 32 devices: a whole 2x2x4 slice. The times are simulated.
32 devices in a mesh: dp: 4 (over y, x), px: 4 (over z), py: 2 (over core).
Axes of the slice: x: 2, y: 2, z: 4, core: 2. Of those that a mesh axis runs over, the one named last changes fastest.
Arguments:
- fields: bfloat16 [4, 16, 16, 32, 256], P('dp', 'px', 'py'), may hold values from -6 to 6
- cotangent: bfloat16 [4, 16, 16, 32, 256], P('dp', 'px', 'py'), may hold values from -6 to 6
- first_weight: bfloat16 [6912, 256], replicated, may hold values from -0.078125 to 0.078125
- second_weight: bfloat16 [6912, 256], replicated, may hold values from -0.078125 to 0.078125
Outputs:
- output: bfloat16 [4, 16, 16, 32, 256], P('dp', 'px', 'py')
- field_grad: bfloat16 [4, 16, 16, 32, 256], P('dp', 'px', 'py')
- first_grad: float32 [6912, 256], P('dp', ('px', 'py'))
- second_grad: float32 [6912, 256], P('dp', ('px', 'py'))
All inputs are finite; a program needn't handle non-finite values.
Results may differ from a plain program's by a relative error of at most 0.0033.
Values may be sent and summed in bfloat16 or wider, within the bound.
A program may use at most 128 MiB of HBM per device.

v0:
```python
import jax
import jax.numpy as jnp
from jax import lax
from jax.sharding import PartitionSpec as P


def with_halo(block, sides, width):
    for axis, dim in sides:
        count = lax.axis_size(axis)
        forward = [(i, i + 1) for i in range(count - 1)]
        backward = [(target, source) for source, target in forward]
        low = lax.ppermute(
            lax.slice_in_dim(block, block.shape[dim] - width, None, axis=dim), axis, forward
        )
        high = lax.ppermute(lax.slice_in_dim(block, 0, width, axis=dim), axis, backward)
        block = jnp.concatenate([low, block, high], axis=dim)
    return block


def gelu_tanh(v):
    return jax.nn.gelu(v, approximate=True)


def pad_faces(field):
    padded = with_halo(field, (("px", 1), ("py", 2)), 1)
    return jnp.pad(padded, ((0, 0), (0, 0), (0, 0), (1, 1), (0, 0)))


def window(padded, start_x, start_y, start_z):
    batch, size_x, size_y, size_z, width = padded.shape
    block = padded[
        :,
        start_x : start_x + size_x - 2,
        start_y : start_y + size_y - 2,
        start_z : start_z + size_z - 2,
        :,
    ]
    return block.reshape(-1, width)


def conv(padded, weight, flipped):
    width = padded.shape[-1]
    total = None
    for offset in range(27):
        first, second, third = (offset // 9, offset // 3 % 3, offset % 3)
        block = weight[offset * width : (offset + 1) * width]
        if flipped:
            rows = window(padded, 2 - first, 2 - second, 2 - third)
            term = lax.dot_general(
                rows, block, (((1,), (1,)), ((), ())), preferred_element_type=jnp.float32
            )
        else:
            rows = window(padded, first, second, third)
            term = jnp.dot(rows, block, preferred_element_type=jnp.float32)
        total = term if total is None else total + term
    return total


def weight_terms(padded, grads):
    blocks = []
    for offset in range(27):
        first, second, third = (offset // 9, offset // 3 % 3, offset % 3)
        rows = window(padded, first, second, third)
        blocks.append(
            lax.dot_general(
                rows, grads, (((0,), (0,)), ((), ())), preferred_element_type=jnp.float32
            )
        )
    return jnp.concatenate(blocks, axis=0)


def body(fields, cotangent, first_weight, second_weight):
    shape = fields.shape
    width = shape[-1]
    rollouts = shape[0] * lax.axis_size("dp")
    fields_padded = pad_faces(fields)
    pre = conv(fields_padded, first_weight, False)
    hidden = gelu_tanh(pre).astype(jnp.bfloat16)
    hidden_padded = pad_faces(hidden.reshape(shape))
    second_out = conv(hidden_padded, second_weight, False)
    output = (
        (fields.reshape(-1, width).astype(jnp.float32) + second_out)
        .astype(jnp.bfloat16)
        .reshape(shape)
    )
    cot_flat = cotangent.reshape(-1, width)
    cot_padded = pad_faces(cotangent)
    hidden_grad = conv(cot_padded, second_weight, True)
    second_terms = weight_terms(hidden_padded, cot_flat) / rollouts
    gelu_back = jax.vjp(gelu_tanh, pre)[1]
    pre_grad = gelu_back(hidden_grad)[0].astype(jnp.bfloat16)
    pre_padded = pad_faces(pre_grad.reshape(shape))
    field_term = conv(pre_padded, first_weight, True)
    field_grad = (cot_flat.astype(jnp.float32) + field_term).astype(jnp.bfloat16).reshape(shape)
    first_terms = weight_terms(fields_padded, pre_grad) / rollouts
    partial_sums = (
        lax.psum_scatter(first_terms, "dp", scatter_dimension=0, tiled=True),
        lax.psum_scatter(second_terms, "dp", scatter_dimension=0, tiled=True),
    )
    first_grad, second_grad = (
        lax.psum_scatter(partial_sums[0], ("px", "py"), scatter_dimension=1, tiled=True),
        lax.psum_scatter(partial_sums[1], ("px", "py"), scatter_dimension=1, tiled=True),
    )
    return (output, field_grad, first_grad, second_grad)


def solution(mesh):
    placed = (P("dp", "px", "py", None, None), P("dp", "px", "py", None, None), P(), P())
    return jax.shard_map(
        body,
        mesh=mesh,
        in_specs=placed,
        out_specs=(
            P("dp", "px", "py", None, None),
            P("dp", "px", "py", None, None),
            P("dp", ("px", "py")),
            P("dp", ("px", "py")),
        ),
        check_vma=False,
    )
```

profile of v0, /device:TPU:0, one launch (start us, length us, event | category | flops | bytes accessed | tf_op | source)
XLA Modules:
  0.0 313.6 jit_solution(10063022050589989901)
XLA Ops:
  8.3 5.0 %collective-permute-start = (bf16[1,1,8,32,256]{4,3,2,1,0:T(8,128)(2,1)S(1)}, bf16[1,1,8,32,256]{4,3,2,1,0:T(8,128)(2,1)S(1)}, u32[]{:S(2)}, u32[]{:S(2)}) collective-permute-start(bf16[1,1,8,32,256]{4,3,2,1,0:T(8,128)(2,1)S(1)} %get-tuple-element.143), channel_id=1, source_target_pairs={{0,2},{2,4},{4,6},{1,3},{3,5},{5,7},{8,10},{10,12},{12,14},{9,11},... | collective-permute-start | bytes 393224 | tf_op jit(solution)/shard_map/ppermute | solution.py:12
  15.5 4.6 %collective-permute-start.8 = (bf16[1,1,8,32,256]{4,3,2,1,0:T(8,128)(2,1)S(1)}, bf16[1,1,8,32,256]{4,3,2,1,0:T(8,128)(2,1)S(1)}, u32[]{:S(2)}, u32[]{:S(2)}) collective-permute-start(bf16[1,1,8,32,256]{4,3,2,1,0:T(8,128)(2,1)S(1)} %get-tuple-element.134), channel_id=1, source_target_pairs={{0,2},{2,4},{4,6},{1,3},{3,5},{5,7},{8,10},{10,12},{12,14},{9,11},... | collective-permute-start | bytes 393224 | tf_op jit(solution)/shard_map/ppermute | solution.py:12
  21.4 1.7 pad_maximum_fusion.11
  28.1 1.9 collective-permute-start.10
  32.1 3.0 fusion.274
  37.3 3.3 %fusion.272 = (bf16[1,4,8,32,256]{4,3,2,1,0:T(8,128)(2,1)S(1)}, bf16[1,4,8,32,256]{4,3,2,1,0:T(8,128)(2,1)S(1)}, bf16[1,4,8,32,256]{4,3,2,1,0:T(8,128)(2,1)S(1)}...) fusion(bf16[1,6,10,34,256]{4,3,2,1,0:T(8,128)(2,1)S(1)} %select, ...), kind=kLoop, calls=%fused_computation.477 | loop fusion | bytes 18874368 | tf_op jit(solution)/shard_map/slice | solution.py:31
  69.5 3.4 %broadcast_multiply_fusion.1 = f32[6912,256]{1,0:T(8,128)} fusion(f32[6912,256]{1,0:T(8,128)S(1)} %convolution_dynamic-update-slice_fusion), kind=kLoop, calls=%fused_computation.3 | loop fusion | flops 1769472 | bytes 14155776 | tf_op jit(solution)/shard_map/div | solution.py:95
  73.0 4.5 %collective-permute-start.4 = (bf16[1,1,8,32,256]{4,3,2,1,0:T(8,128)(2,1)S(1)}, bf16[1,1,8,32,256]{4,3,2,1,0:T(8,128)(2,1)S(1)}, u32[]{:S(2)}, u32[]{:S(2)}) collective-permute-start(bf16[1,1,8,32,256]{4,3,2,1,0:T(8,128)(2,1)S(1)} %get-tuple-element.137), channel_id=1, source_target_pairs={{0,2},{2,4},{4,6},{1,3},{3,5},{5,7},{8,10},{10,12},{12,14},{9,11},... | collective-permute-start | bytes 393224 | tf_op jit(solution)/shard_map/ppermute | solution.py:12
  78.9 2.4 collective-permute-done.4
  81.2 4.5 %collective-permute-done.5 = bf16[1,1,8,32,256]{4,3,2,1,0:T(8,128)(2,1)S(1)} collective-permute-done((bf16[1,1,8,32,256]{4,3,2,1,0:T(8,128)(2,1)S(1)}, bf16[1,1,8,32,256]{4,3,2,1,0:T(8,128)(2,1)S(1)}, u32[]{:S(2)}, u32[]{:S(2)}) %collective-permute-start.5) | collective-permute-done | bytes 131104 | tf_op jit(solution)/shard_map/ppermute | solution.py:15
  85.8 2.0 collective-permute-start.6
  87.8 1.8 collective-permute-start.7
  101.5 3.3 %broadcast_multiply_fusion = f32[6912,256]{1,0:T(8,128)} fusion(f32[6912,256]{1,0:T(8,128)S(1)} %fusion.27), kind=kLoop, calls=%fused_computation.2 | loop fusion | flops 1769472 | bytes 14155776 | tf_op jit(solution)/shard_map/div | solution.py:89
  104.9 3.5 %collective-permute-start.12 = (bf16[1,1,8,32,256]{4,3,2,1,0:T(8,128)(2,1)S(1)}, bf16[1,1,8,32,256]{4,3,2,1,0:T(8,128)(2,1)S(1)}, u32[]{:S(2)}, u32[]{:S(2)}) collective-permute-start(bf16[1,1,8,32,256]{4,3,2,1,0:T(8,128)(2,1)S(1)} %get-tuple-element.128), channel_id=1, source_target_pairs={{0,2},{2,4},{4,6},{1,3},{3,5},{5,7},{8,10},{10,12},{12,14},{9,11},... | collective-permute-start | bytes 393224 | tf_op jit(solution)/shard_map/ppermute | solution.py:12
  109.6 1.8 collective-permute-done.12
  111.4 4.1 %collective-permute-done.13 = bf16[1,1,8,32,256]{4,3,2,1,0:T(8,128)(2,1)S(1)} collective-permute-done((bf16[1,1,8,32,256]{4,3,2,1,0:T(8,128)(2,1)S(1)}, bf16[1,1,8,32,256]{4,3,2,1,0:T(8,128)(2,1)S(1)}, u32[]{:S(2)}, u32[]{:S(2)}) %collective-permute-start.13) | collective-permute-done | bytes 131104 | tf_op jit(solution)/shard_map/ppermute | solution.py:15
  116.8 1.5 collective-permute-start.15
  120.9 3.5 %fusion.271 = (bf16[1,4,8,32,256]{4,3,2,1,0:T(8,128)(2,1)}, bf16[1,4,8,32,256]{4,3,2,1,0:T(8,128)(2,1)}, bf16[1,4,8,32,256]{4,3,2,1,0:T(8,128)(2,1)}, bf16[1,4,8...) fusion(bf16[1,6,10,34,256]{4,3,2,1,0:T(8,128)(2,1)S(1)} %select, ...), kind=kLoop, calls=%fused_computation.476 | loop fusion | bytes 18874368 | tf_op jit(solution)/shard_map/slice | solution.py:31
  125.1 4.2 %fusion.273 = (bf16[1,4,8,32,256]{4,3,2,1,0:T(8,128)(2,1)}, bf16[1,4,8,32,256]{4,3,2,1,0:T(8,128)(2,1)}, bf16[1,4,8,32,256]{4,3,2,1,0:T(8,128)(2,1)}, bf16[1,4,8...) fusion(bf16[1,6,10,34,256]{4,3,2,1,0:T(8,128)(2,1)S(1)} %select, ...), kind=kLoop, calls=%fused_computation.478 | loop fusion | bytes 18874368 | tf_op jit(solution)/shard_map/slice | solution.py:31
  141.2 11.5 %reduce-scatter.9.cloned.1.call-done = f32[1728,256]{1,0:T(8,128)} async-done(((f32[6912,256]{1,0:T(8,128)}), f32[1728,256]{1,0:T(8,128)}) %reduce-scatter.9.cloned.1.call-update) | async-done | bytes 1769488 | tf_op jit(solution)/shard_map/reduce_scatter | solution.py:97
  152.8 2.8 copy.39
  155.8 1.5 convolution_add_fusion.11
  157.3 1.4 fusion.192
  161.4 1.4 convolution_add_fusion.8
  172.0 2.0 fusion.16
  174.0 58.4 %reduce-scatter.11.cloned.1.call-done = f32[1728,256]{1,0:T(8,128)} async-done(((f32[6912,256]{1,0:T(8,128)}), f32[1728,256]{1,0:T(8,128)}) %reduce-scatter.11.cloned.1.call-update) | async-done | bytes 1769488 | tf_op jit(solution)/shard_map/reduce_scatter | solution.py:98
  232.4 2.7 copy.41
  235.1 1.4 convolution_add_fusion.57
  237.9 1.4 convolution_add_fusion.56
  250.8 2.0 fusion.15
  252.8 18.0 %reduce-scatter.13.cloned.1.call-done = f32[32,1728]{1,0:T(8,128)} async-done(((f32[256,1728]{1,0:T(8,128)}), f32[32,1728]{1,0:T(8,128)}) %reduce-scatter.13.cloned.1.call-update) | async-done | bytes 221200
  270.8 36.1 %reduce-scatter.15.cloned.1.call-done = f32[32,1728]{1,0:T(8,128)} async-done(((f32[256,1728]{1,0:T(8,128)}), f32[32,1728]{1,0:T(8,128)}) %reduce-scatter.15.cloned.1.call-update) | async-done | bytes 221200
  (298 shorter events, 97.2 us)
Async XLA Ops:
  7.2 19.8 %copy-start.9 = (bf16[1,4,8,32,256]{4,3,2,1,0:T(8,128)(2,1)S(1)}, bf16[1,4,8,32,256]{4,3,2,1,0:T(8,128)(2,1)}, u32[]{:S(2)}) copy-start(bf16[1,4,8,32,256]{4,3,2,1,0:T(8,128)(2,1)} %param.5) | copy-start | bytes 1572868
  7.2 145.6 %reduce-scatter.9.cloned.1.call-start = ((), (), s32[]{:S(2)}) async-start(), calls=%async_computation.4 | async-start | bytes 8847360 | tf_op jit(solution)/shard_map/reduce_scatter | solution.py:97
  8.3 13.1 %collective-permute-start = (bf16[1,1,8,32,256]{4,3,2,1,0:T(8,128)(2,1)S(1)}, bf16[1,1,8,32,256]{4,3,2,1,0:T(8,128)(2,1)S(1)}, u32[]{:S(2)}, u32[]{:S(2)}) collective-permute-start(bf16[1,1,8,32,256]{4,3,2,1,0:T(8,128)(2,1)S(1)} %get-tuple-element.143), channel_id=1, source_target_pairs={{0,2},{2,4},{4,6},{1,3},{3,5},{5,7},{8,10},{10,12},{12,14},{9,11},... | collective-permute-start | bytes 393224 | tf_op jit(solution)/shard_map/ppermute | solution.py:12
  13.2 8.2 %collective-permute-start.1 = (bf16[1,1,8,32,256]{4,3,2,1,0:T(8,128)(2,1)S(1)}, bf16[1,1,8,32,256]{4,3,2,1,0:T(8,128)(2,1)S(1)}, u32[]{:S(2)}, u32[]{:S(2)}) collective-permute-start(bf16[1,1,8,32,256]{4,3,2,1,0:T(8,128)(2,1)S(1)} %get-tuple-element.142), channel_id=1, source_target_pairs={{2,0},{4,2},{6,4},{3,1},{5,3},{7,5},{10,8},{12,10},{14,12},{11,9},... | collective-permute-start | bytes 393224 | tf_op jit(solution)/shard_map/ppermute | solution.py:15
  15.5 10.3 %collective-permute-start.8 = (bf16[1,1,8,32,256]{4,3,2,1,0:T(8,128)(2,1)S(1)}, bf16[1,1,8,32,256]{4,3,2,1,0:T(8,128)(2,1)S(1)}, u32[]{:S(2)}, u32[]{:S(2)}) collective-permute-start(bf16[1,1,8,32,256]{4,3,2,1,0:T(8,128)(2,1)S(1)} %get-tuple-element.134), channel_id=1, source_target_pairs={{0,2},{2,4},{4,6},{1,3},{3,5},{5,7},{8,10},{10,12},{12,14},{9,11},... | collective-permute-start | bytes 393224 | tf_op jit(solution)/shard_map/ppermute | solution.py:12
  20.1 6.9 %collective-permute-start.9 = (bf16[1,1,8,32,256]{4,3,2,1,0:T(8,128)(2,1)S(1)}, bf16[1,1,8,32,256]{4,3,2,1,0:T(8,128)(2,1)S(1)}, u32[]{:S(2)}, u32[]{:S(2)}) collective-permute-start(bf16[1,1,8,32,256]{4,3,2,1,0:T(8,128)(2,1)S(1)} %get-tuple-element.133), channel_id=1, source_target_pairs={{2,0},{4,2},{6,4},{3,1},{5,3},{7,5},{10,8},{12,10},{14,12},{11,9},... | collective-permute-start | bytes 393224 | tf_op jit(solution)/shard_map/ppermute | solution.py:15
  23.1 21.3 %copy-start.38 = (bf16[1,4,8,32,256]{4,3,2,1,0:T(8,128)(2,1)}, bf16[1,4,8,32,256]{4,3,2,1,0:T(8,128)(2,1)S(1)}, u32[]{:S(2)}) copy-start(bf16[1,4,8,32,256]{4,3,2,1,0:T(8,128)(2,1)S(1)} %get-tuple-element.141) | copy-start | bytes 1572868
  23.1 26.3 %copy-start.36 = (bf16[1,4,8,32,256]{4,3,2,1,0:T(8,128)(2,1)}, bf16[1,4,8,32,256]{4,3,2,1,0:T(8,128)(2,1)S(1)}, u32[]{:S(2)}) copy-start(bf16[1,4,8,32,256]{4,3,2,1,0:T(8,128)(2,1)S(1)} %get-tuple-element.139) | copy-start | bytes 1572868
  23.2 8.2 %collective-permute-start.2 = (bf16[1,6,1,32,256]{4,3,2,1,0:T(8,128)(2,1)S(1)}, bf16[1,6,1,32,256]{4,3,2,1,0:T(8,128)(2,1)S(1)}, u32[]{:S(2)}, u32[]{:S(2)}) collective-permute-start(bf16[1,6,1,32,256]{4,3,2,1,0:T(8,128)(2,1)S(1)} %get-tuple-element.124), channel_id=1, source_target_pairs={{0,1},{2,3},{4,5},{6,7},{8,9},{10,11},{12,13},{14,15},{16,17},{18,... | collective-permute-start | bytes 294920 | tf_op jit(solution)/shard_map/ppermute | solution.py:12
  24.5 6.9 %collective-permute-start.3 = (bf16[1,6,1,32,256]{4,3,2,1,0:T(8,128)(2,1)S(1)}, bf16[1,6,1,32,256]{4,3,2,1,0:T(8,128)(2,1)S(1)}, u32[]{:S(2)}, u32[]{:S(2)}) collective-permute-start(bf16[1,6,1,32,256]{4,3,2,1,0:T(8,128)(2,1)S(1)} %get-tuple-element.125), channel_id=1, source_target_pairs={{1,0},{3,2},{5,4},{7,6},{9,8},{11,10},{13,12},{15,14},{17,16},{19,... | collective-permute-start | bytes 294920 | tf_op jit(solution)/shard_map/ppermute | solution.py:15
  28.1 8.4 %collective-permute-start.10 = (bf16[1,6,1,32,256]{4,3,2,1,0:T(8,128)(2,1)S(1)}, bf16[1,6,1,32,256]{4,3,2,1,0:T(8,128)(2,1)S(1)}, u32[]{:S(2)}, u32[]{:S(2)}) collective-permute-start(bf16[1,6,1,32,256]{4,3,2,1,0:T(8,128)(2,1)S(1)} %get-tuple-element.115), channel_id=1, source_target_pairs={{0,1},{2,3},{4,5},{6,7},{8,9},{10,11},{12,13},{14,15},{16,17},{18,... | collective-permute-start | bytes 294920 | tf_op jit(solution)/shard_map/ppermute | solution.py:12
  30.0 6.5 %collective-permute-start.11 = (bf16[1,6,1,32,256]{4,3,2,1,0:T(8,128)(2,1)S(1)}, bf16[1,6,1,32,256]{4,3,2,1,0:T(8,128)(2,1)S(1)}, u32[]{:S(2)}, u32[]{:S(2)}) collective-permute-start(bf16[1,6,1,32,256]{4,3,2,1,0:T(8,128)(2,1)S(1)} %get-tuple-element.116), channel_id=1, source_target_pairs={{1,0},{3,2},{5,4},{7,6},{9,8},{11,10},{13,12},{15,14},{17,16},{19,... | collective-permute-start | bytes 294920 | tf_op jit(solution)/shard_map/ppermute | solution.py:15
  43.5 5.3 %copy-start.42 = (bf16[1,4,8,32,256]{4,3,2,1,0:T(8,128)(2,1)}, bf16[1,4,8,32,256]{4,3,2,1,0:T(8,128)(2,1)S(1)}, u32[]{:S(2)}) copy-start(bf16[1,4,8,32,256]{4,3,2,1,0:T(8,128)(2,1)S(1)} %get-tuple-element.123) | copy-start | bytes 1572868
  72.9 159.5 %reduce-scatter.11.cloned.1.call-start = ((), (), s32[]{:S(2)}) async-start(), calls=%async_computation.5 | async-start | bytes 8847360 | tf_op jit(solution)/shard_map/reduce_scatter | solution.py:98
  73.0 8.2 %collective-permute-start.4 = (bf16[1,1,8,32,256]{4,3,2,1,0:T(8,128)(2,1)S(1)}, bf16[1,1,8,32,256]{4,3,2,1,0:T(8,128)(2,1)S(1)}, u32[]{:S(2)}, u32[]{:S(2)}) collective-permute-start(bf16[1,1,8,32,256]{4,3,2,1,0:T(8,128)(2,1)S(1)} %get-tuple-element.137), channel_id=1, source_target_pairs={{0,2},{2,4},{4,6},{1,3},{3,5},{5,7},{8,10},{10,12},{12,14},{9,11},... | collective-permute-start | bytes 393224 | tf_op jit(solution)/shard_map/ppermute | solution.py:12
  77.6 8.2 %collective-permute-start.5 = (bf16[1,1,8,32,256]{4,3,2,1,0:T(8,128)(2,1)S(1)}, bf16[1,1,8,32,256]{4,3,2,1,0:T(8,128)(2,1)S(1)}, u32[]{:S(2)}, u32[]{:S(2)}) collective-permute-start(bf16[1,1,8,32,256]{4,3,2,1,0:T(8,128)(2,1)S(1)} %get-tuple-element.138), channel_id=1, source_target_pairs={{2,0},{4,2},{6,4},{3,1},{5,3},{7,5},{10,8},{12,10},{14,12},{11,9},... | collective-permute-start | bytes 393224 | tf_op jit(solution)/shard_map/ppermute | solution.py:15
  85.8 3.9 %collective-permute-start.6 = (bf16[1,6,1,32,256]{4,3,2,1,0:T(8,128)(2,1)S(1)}, bf16[1,6,1,32,256]{4,3,2,1,0:T(8,128)(2,1)S(1)}, u32[]{:S(2)}, u32[]{:S(2)}) collective-permute-start(bf16[1,6,1,32,256]{4,3,2,1,0:T(8,128)(2,1)S(1)} %get-tuple-element.119), channel_id=1, source_target_pairs={{0,1},{2,3},{4,5},{6,7},{8,9},{10,11},{12,13},{14,15},{16,17},{18,... | collective-permute-start | bytes 294920 | tf_op jit(solution)/shard_map/ppermute | solution.py:12
  87.8 3.2 %collective-permute-start.7 = (bf16[1,6,1,32,256]{4,3,2,1,0:T(8,128)(2,1)S(1)}, bf16[1,6,1,32,256]{4,3,2,1,0:T(8,128)(2,1)S(1)}, u32[]{:S(2)}, u32[]{:S(2)}) collective-permute-start(bf16[1,6,1,32,256]{4,3,2,1,0:T(8,128)(2,1)S(1)} %get-tuple-element.120), channel_id=1, source_target_pairs={{1,0},{3,2},{5,4},{7,6},{9,8},{11,10},{13,12},{15,14},{17,16},{19,... | collective-permute-start | bytes 294920 | tf_op jit(solution)/shard_map/ppermute | solution.py:15
  89.7 10.0 %copy-start.31 = (bf16[1,4,8,32,256]{4,3,2,1,0:T(8,128)(2,1)}, bf16[1,4,8,32,256]{4,3,2,1,0:T(8,128)(2,1)S(1)}, u32[]{:S(2)}) copy-start(bf16[1,4,8,32,256]{4,3,2,1,0:T(8,128)(2,1)S(1)} %get-tuple-element.135) | copy-start | bytes 1572868
  91.2 7.5 %copy-start.7 = (bf16[1,6,9,32,256]{4,3,2,1,0:T(8,128)(2,1)}, bf16[1,6,9,32,256]{4,3,2,1,0:T(8,128)(2,1)S(1)}, u32[]{:S(2)}) copy-start(bf16[1,6,9,32,256]{4,3,2,1,0:T(8,128)(2,1)S(1)} %get-tuple-element.118) | copy-start | bytes 2654212
  91.2 9.6 %copy-start.5 = (bf16[1,6,9,32,256]{4,3,2,1,0:T(8,128)(2,1)}, bf16[1,6,9,32,256]{4,3,2,1,0:T(8,128)(2,1)S(1)}, u32[]{:S(2)}) copy-start(bf16[1,6,9,32,256]{4,3,2,1,0:T(8,128)(2,1)S(1)} %get-tuple-element.117) | copy-start | bytes 2654212
  104.8 166.0 %reduce-scatter.13.cloned.1.call-start = ((), (), s32[]{:S(2)}) async-start(), calls=%async_computation.6 | async-start | bytes 2064384
  104.9 6.5 %collective-permute-start.12 = (bf16[1,1,8,32,256]{4,3,2,1,0:T(8,128)(2,1)S(1)}, bf16[1,1,8,32,256]{4,3,2,1,0:T(8,128)(2,1)S(1)}, u32[]{:S(2)}, u32[]{:S(2)}) collective-permute-start(bf16[1,1,8,32,256]{4,3,2,1,0:T(8,128)(2,1)S(1)} %get-tuple-element.128), channel_id=1, source_target_pairs={{0,2},{2,4},{4,6},{1,3},{3,5},{5,7},{8,10},{10,12},{12,14},{9,11},... | collective-permute-start | bytes 393224 | tf_op jit(solution)/shard_map/ppermute | solution.py:12
  108.3 7.2 %collective-permute-start.13 = (bf16[1,1,8,32,256]{4,3,2,1,0:T(8,128)(2,1)S(1)}, bf16[1,1,8,32,256]{4,3,2,1,0:T(8,128)(2,1)S(1)}, u32[]{:S(2)}, u32[]{:S(2)}) collective-permute-start(bf16[1,1,8,32,256]{4,3,2,1,0:T(8,128)(2,1)S(1)} %get-tuple-element.129), channel_id=1, source_target_pairs={{2,0},{4,2},{6,4},{3,1},{5,3},{7,5},{10,8},{12,10},{14,12},{11,9},... | collective-permute-start | bytes 393224 | tf_op jit(solution)/shard_map/ppermute | solution.py:15
  115.5 3.7 %collective-permute-start.14 = (bf16[1,6,1,32,256]{4,3,2,1,0:T(8,128)(2,1)S(1)}, bf16[1,6,1,32,256]{4,3,2,1,0:T(8,128)(2,1)S(1)}, u32[]{:S(2)}, u32[]{:S(2)}) collective-permute-start(bf16[1,6,1,32,256]{4,3,2,1,0:T(8,128)(2,1)S(1)} %get-tuple-element.110), channel_id=1, source_target_pairs={{0,1},{2,3},{4,5},{6,7},{8,9},{10,11},{12,13},{14,15},{16,17},{18,... | collective-permute-start | bytes 294920 | tf_op jit(solution)/shard_map/ppermute | solution.py:12
  116.8 3.2 %collective-permute-start.15 = (bf16[1,6,1,32,256]{4,3,2,1,0:T(8,128)(2,1)S(1)}, bf16[1,6,1,32,256]{4,3,2,1,0:T(8,128)(2,1)S(1)}, u32[]{:S(2)}, u32[]{:S(2)}) collective-permute-start(bf16[1,6,1,32,256]{4,3,2,1,0:T(8,128)(2,1)S(1)} %get-tuple-element.111), channel_id=1, source_target_pairs={{1,0},{3,2},{5,4},{7,6},{9,8},{11,10},{13,12},{15,14},{17,16},{19,... | collective-permute-start | bytes 294920 | tf_op jit(solution)/shard_map/ppermute | solution.py:15
  125.0 4.3 %copy-start.3 = (bf16[6912,256]{1,0:T(8,128)(2,1)S(1)}, bf16[6912,256]{1,0:T(8,128)(2,1)}, u32[]{:S(2)}) copy-start(bf16[6912,256]{1,0:T(8,128)(2,1)} %param.7) | copy-start | bytes 10616836
  141.2 14.6 %copy-start.10 = (f32[1024,256]{1,0:T(8,128)S(1)}, f32[1024,256]{1,0:T(8,128)}, u32[]{:S(2)}) copy-start(f32[1024,256]{1,0:T(8,128)} %convolution_add_fusion.12) | copy-start | bytes 3145732
  155.6 151.3 %reduce-scatter.15.cloned.1.call-start = ((), (), s32[]{:S(2)}) async-start(), calls=%async_computation.7 | async-start | bytes 2064384
  155.8 4.3 %copy-start.30 = (bf16[1,4,8,32,256]{4,3,2,1,0:T(8,128)(2,1)S(1)}, bf16[1,4,8,32,256]{4,3,2,1,0:T(8,128)(2,1)}, u32[]{:S(2)}) copy-start(bf16[1,4,8,32,256]{4,3,2,1,0:T(8,128)(2,1)} %get-tuple-element.85) | copy-start | bytes 1572868
  174.0 62.5 %copy-start.11 = (bf16[1,4,8,32,256]{4,3,2,1,0:T(8,128)(2,1)S(1)}, bf16[1,4,8,32,256]{4,3,2,1,0:T(8,128)(2,1)}, u32[]{:S(2)}) copy-start(bf16[1,4,8,32,256]{4,3,2,1,0:T(8,128)(2,1)} %get-tuple-element.50) | copy-start | bytes 1572868
  235.1 4.1 %copy-start.28 = (bf16[1,4,8,32,256]{4,3,2,1,0:T(8,128)(2,1)S(1)}, bf16[1,4,8,32,256]{4,3,2,1,0:T(8,128)(2,1)}, u32[]{:S(2)}) copy-start(bf16[1,4,8,32,256]{4,3,2,1,0:T(8,128)(2,1)} %get-tuple-element.97) | copy-start | bytes 1572868
  (33 other events, 94.0 us)
Sparse Core Ops, SparseCore 0:
  73.0 79.6 reduce-scatter.8
  155.8 76.5 reduce-scatter.10
  235.3 35.4 reduce-scatter.12
  273.6 33.2 reduce-scatter.14
where the time goes:
time: 320 us; the launch traced here: 314 us
  waiting for transfers between devices  140 us (44%)
  matrix products  82.8 us (26%)
  starting transfers between devices  35.4 us (11%)
  local copies, waits for them, and re-layouts  25.3 us (8%)
  between operations  16 us (5%)
  other arithmetic  14.1 us (4%)
    reduce_scatter x1, waiting for transfers between devices, body(): lax.psum_scatter(second_terms, 'dp', scatter_dimension=0, tiled=True)  58.4 us
    unnamed x6, waiting for transfers between devices  54.2 us
    dot_general x54, matrix products, conv(): lax.dot_general(rows, block, (((1,), (1,)), ((), ())), preferred_element_...  34 us
    dot_general x54, matrix products, conv(): term = jnp.dot(rows, block, preferred_element_type=jnp.float32)  29.9 us
    ppermute x8, starting transfers between devices, with_halo(): lax.ppermute(lax.slice_in_dim(block, block.shape[dim] - width, None, axis...  24.1 us
    dot_general x54, matrix products, weight_terms(): lax.dot_general(rows, grads, (((0,), (0,)), ((), ())), preferred_element_...  18.9 us
    slice x6, local copies, waits for them, and re-layouts, window(): padded[:, start_x:start_x + size_x - 2, start_y:start_y + size_y - 2, sta...  16.5 us
    ppermute x8, waiting for transfers between devices, with_halo(): lax.ppermute(lax.slice_in_dim(block, 0, width, axis=dim), axis, backward)  11.9 us
  transfers between devices with their start and end apart: 20, of which 11 were waited for; matrix products, arithmetic and copies ran while one was open for 27% of the time, Pallas kernels for 0%

commit v1 on v0

v1 whole, which is shorter than its diff:
```python
import functools

import jax
import jax.numpy as jnp
from jax import lax
from jax.experimental import pallas as pl
from jax.experimental.pallas import tpu as pltpu
from jax.sharding import PartitionSpec as P

MESH = pl.DeviceIdType.MESH
F32, BF16 = jnp.float32, jnp.bfloat16
DIRS = [(dx, dy) for dx in (-1, 0, 1) for dy in (-1, 0, 1) if dx or dy]
GELU_C = 0.7978845608028654
GELU_A = 0.044715


def gelu_parts(v):
    return jnp.tanh(GELU_C * (v + GELU_A * (v * v * v)))


def kernel(
    sizes,
    fields, cot, w1_hbm, w2_hbm,
    out_ref, fgrad_ref, g1_ref, g2_ref,
    w1, w2, p_f, p_c, p_h, p_g, z_a, z_b, z_c, lhs_f, lhs_h, pre,
    own, send_a, recv_a, recv_b, tot, send_z, recv_z,
    sem_w, halo_send, halo_recv, a_send, a_recv, b_send, b_recv, z_send, z_recv,
):
    ndp, npx, npy, rollouts = sizes
    nx, ny, nz, ch = fields.shape
    cells = nx * ny * nz
    half = ch // npy
    rows = own.shape[1] // ndp
    rpad = tot.shape[0]
    wid = recv_z.shape[2]
    nj = half // wid
    d, x, y = lax.axis_index("dp"), lax.axis_index("px"), lax.axis_index("py")

    load_w = [
        pltpu.make_async_copy(w1_hbm, w1, sem_w.at[0]),
        pltpu.make_async_copy(w2_hbm, w2, sem_w.at[1]),
    ]
    for copy in load_w:
        copy.start()

    barrier = pltpu.get_barrier_semaphore()
    for i in range(1, ndp):
        pl.semaphore_signal(
            barrier, inc=1, device_id=(lax.rem(d + i, ndp), x, y), device_id_type=MESH
        )
    for i in range(1, npx * npy):
        other = lax.rem(x * npy + y + i, npx * npy)
        pl.semaphore_signal(
            barrier, inc=1, device_id=(d, other // npy, lax.rem(other, npy)), device_id_type=MESH
        )
    pl.semaphore_wait(barrier, ndp - 1 + npx * npy - 1)

    def exists(dx, dy):
        return (x + dx >= 0) & (x + dx < npx) & (y + dy >= 0) & (y + dy < npy)

    def span_src(step, size, base):
        if step == 0:
            return pl.ds(base, size)
        return pl.ds(base if step < 0 else base + size - 1, 1)

    def span_dst(step, size):
        if step == 0:
            return pl.ds(1, size)
        return pl.ds(size + 1 if step < 0 else 0, 1)

    def halo_copy(which, src, base, padded, index):
        dx, dy = DIRS[index]
        return pltpu.make_async_remote_copy(
            src_ref=src.at[span_src(dx, nx, base), span_src(dy, ny, base)],
            dst_ref=padded.at[span_dst(dx, nx), span_dst(dy, ny)],
            send_sem=halo_send.at[which, index],
            recv_sem=halo_recv.at[which, index],
            device_id=(d, x + dx, y + dy),
            device_id_type=MESH,
        )

    def halo_start(which, src, base, padded):
        for index, (dx, dy) in enumerate(DIRS):
            @pl.when(exists(dx, dy))
            def _():
                halo_copy(which, src, base, padded, index).start()

            @pl.when(jnp.logical_not(exists(-dx, -dy)))
            def _():
                sx, sy = span_dst(dx, nx), span_dst(dy, ny)
                padded[sx, sy] = jnp.zeros((sx.size, sy.size, nz, ch), BF16)

    def halo_wait(which, src, base, padded):
        for index, (dx, dy) in enumerate(DIRS):
            @pl.when(exists(dx, dy))
            def _():
                halo_copy(which, src, base, padded, index).wait_send()

            @pl.when(exists(-dx, -dy))
            def _():
                halo_copy(which, src, base, padded, index).wait_recv()

    def build(padded, shifted):
        @pl.loop(0, nx + 2)
        def _(i):
            plane = padded[i]
            flat = plane.reshape((ny + 2) * nz, ch).astype(F32)
            place = lax.broadcasted_iota(jnp.int32, flat.shape, 0) % nz
            low = jnp.where(place == 0, 0.0, pltpu.roll(flat, 1, 0))
            high = jnp.where(place == nz - 1, 0.0, pltpu.roll(flat, flat.shape[0] - 1, 0))
            shifted[i, :, :, 0:ch] = low.astype(BF16).reshape(plane.shape)
            shifted[i, :, :, ch : 2 * ch] = plane
            shifted[i, :, :, 2 * ch : 3 * ch] = high.astype(BF16).reshape(plane.shape)

    tile = ny * nz

    def conv(shifted, weight, flipped, finish):
        @pl.loop(0, nx)
        def _(i):
            total = None
            for a in range(3):
                for b in range(3):
                    first = (9 * a + 3 * b) * ch
                    if not flipped:
                        lhs = shifted[i + a, pl.ds(b, ny)].reshape(tile, 3 * ch)
                        term = jnp.dot(
                            lhs, weight[pl.ds(first, 3 * ch)], preferred_element_type=F32
                        )
                        total = term if total is None else total + term
                        continue
                    for c in range(3):
                        lhs = shifted[
                            i + 2 - a, pl.ds(2 - b, ny), :, pl.ds((2 - c) * ch, ch)
                        ].reshape(tile, ch)
                        term = lax.dot_general(
                            lhs,
                            weight[pl.ds(first + c * ch, ch)],
                            (((1,), (1,)), ((), ())),
                            preferred_element_type=F32,
                        )
                        total = term if total is None else total + term
            finish(i, total)

    partner = 1 - y

    def a_copy(which, step):
        part = pl.ds(pl.multiple_of(step * 3 * ch, 3 * ch), 3 * ch)
        return pltpu.make_async_remote_copy(
            src_ref=send_a.at[which, part],
            dst_ref=recv_a.at[which, part],
            send_sem=a_send.at[which, step],
            recv_sem=a_recv.at[which, step],
            device_id=(d, x, partner),
            device_id_type=MESH,
        )

    def weight_grad(which, lhs, shifted):
        @pl.loop(0, 9)
        def _(step):
            a, b = step // 3, step % 3
            rhs = shifted[pl.ds(2 - a, nx), pl.ds(2 - b, ny)].reshape(cells, 3 * ch)
            prod = jnp.dot(lhs[...], rhs, preferred_element_type=F32)
            for c in range(3):
                block = prod[:, (2 - c) * ch : (3 - c) * ch]
                here = pl.ds(pl.multiple_of(step * 3 * ch, ch) + c * ch, ch)
                low, high = block[:, :half], block[:, half:]
                own[which, here] = jnp.where(y == 0, low, high)
                send_a[which, here] = jnp.where(y == 0, high, low).astype(BF16)
            a_copy(which, step).start()

    def b_copy(which, hop):
        peer = lax.rem(d + hop, ndp)
        return pltpu.make_async_remote_copy(
            src_ref=send_a.at[which, pl.ds(pl.multiple_of(peer * rows, 16), rows)],
            dst_ref=recv_b.at[which, hop - 1],
            send_sem=b_send.at[which, hop - 1],
            recv_sem=b_recv.at[which, hop - 1],
            device_id=(peer, x, y),
            device_id_type=MESH,
        )

    def rows_start(which):
        @pl.loop(0, 9)
        def _(step):
            a_copy(which, step).wait()

        for hop in [*range(1, ndp), 0]:
            peer = lax.rem(d + hop, ndp)
            part = pl.ds(pl.multiple_of(peer * rows, 16), rows)
            total = own[which, part] + recv_a[which, part].astype(F32)
            if hop:
                send_a[which, part] = total.astype(BF16)
                b_copy(which, hop).start()
            else:
                own[which, part] = total

    def z_ids(j):
        owner = y * nj + j
        return owner // npy, lax.rem(owner, npy)

    def z_remote(which, j):
        px_o, py_o = z_ids(j)
        return pltpu.make_async_remote_copy(
            src_ref=send_z.at[which, pl.ds(j * wid, wid)],
            dst_ref=recv_z.at[which, x],
            send_sem=z_send.at[which, j],
            recv_sem=z_recv.at[which, x],
            device_id=(d, px_o, py_o),
            device_id_type=MESH,
        )

    def columns_start(which):
        for hop in range(1, ndp):
            b_copy(which, hop).wait()
        part = pl.ds(pl.multiple_of(d * rows, 16), rows)
        total = own[which, part]
        for hop in range(1, ndp):
            total = total + recv_b[which, hop - 1].astype(F32)
        tot[0:rows] = total
        if rpad > rows:
            tot[rows:rpad] = jnp.zeros((rpad - rows, half), F32)
        send_z[which] = tot[...].T.astype(BF16)
        for j in range(nj):
            px_o, py_o = z_ids(j)
            mine = (px_o == x) & (py_o == y)

            @pl.when(jnp.logical_not(mine))
            def _():
                z_remote(which, j).start()

            @pl.when(mine)
            def _():
                pltpu.make_async_copy(
                    send_z.at[which, pl.ds(j * wid, wid)], recv_z.at[which, x], z_recv.at[which, x]
                ).start()

    def finish_grad(which, grad):
        for j in range(nj):
            px_o, py_o = z_ids(j)

            @pl.when(jnp.logical_not((px_o == x) & (py_o == y)))
            def _():
                z_remote(which, j).wait_send()

        total = None
        for i in range(npx):
            pltpu.make_async_copy(
                recv_z.at[which, i], recv_z.at[which, i], z_recv.at[which, i]
            ).wait()
            term = recv_z[which, i].astype(F32)
            total = term if total is None else total + term
        grad[...] = total / rollouts

    halo_start(0, fields, 0, p_f)
    halo_start(1, cot, 0, p_c)
    p_f[pl.ds(1, nx), pl.ds(1, ny)] = fields[...]
    p_c[pl.ds(1, nx), pl.ds(1, ny)] = cot[...]
    lhs_f[...] = fields[...].reshape(cells, ch).T
    halo_wait(0, fields, 0, p_f)
    build(p_f, z_a)
    load_w[0].wait()

    def hidden_finish(i, total):
        pre[i] = total
        value = (total * (0.5 * (1.0 + gelu_parts(total)))).astype(BF16)
        p_h[i + 1, pl.ds(1, ny)] = value.reshape(ny, nz, ch)

    conv(z_a, w1, False, hidden_finish)
    halo_start(2, p_h, 1, p_h)
    lhs_h[...] = p_h[pl.ds(1, nx), pl.ds(1, ny)].reshape(cells, ch).T
    halo_wait(1, cot, 0, p_c)
    build(p_c, z_b)
    weight_grad(1, lhs_h, z_b)
    rows_start(1)
    load_w[1].wait()

    def grad_finish(i, total):
        v = pre[i]
        t = gelu_parts(v)
        slope = 0.5 * (1.0 + t) + (0.5 * v) * (1.0 - t * t) * (
            GELU_C * (1.0 + (3.0 * GELU_A) * (v * v))
        )
        p_g[i + 1, pl.ds(1, ny)] = (total * slope).astype(BF16).reshape(ny, nz, ch)

    conv(z_b, w2, True, grad_finish)
    halo_start(3, p_g, 1, p_g)
    halo_wait(2, p_h, 1, p_h)
    build(p_h, z_a)

    def out_finish(i, total):
        out_ref[i] = (
            (fields[i].reshape(tile, ch).astype(F32) + total).astype(BF16).reshape(ny, nz, ch)
        )

    conv(z_a, w2, False, out_finish)
    halo_wait(3, p_g, 1, p_g)
    build(p_g, z_c)
    weight_grad(0, lhs_f, z_c)
    rows_start(0)
    columns_start(1)

    def field_finish(i, total):
        fgrad_ref[i] = (
            (cot[i].reshape(tile, ch).astype(F32) + total).astype(BF16).reshape(ny, nz, ch)
        )

    conv(z_c, w1, True, field_finish)
    finish_grad(1, g2_ref)
    columns_start(0)
    finish_grad(0, g1_ref)


def body(sizes, fields, cotangent, first_weight, second_weight):
    ndp, npx, npy = sizes
    batch, nx, ny, nz, ch = fields.shape
    kc = first_weight.shape[0]
    half = ch // npy
    rows = kc // ndp
    rpad = -(-rows // 128) * 128
    wid = ch // (npx * npy)
    cells = nx * ny * nz
    vmem = pl.BlockSpec(memory_space=pltpu.VMEM)
    hbm = pl.BlockSpec(memory_space=pl.ANY)
    padded = pltpu.VMEM((nx + 2, ny + 2, nz, ch), BF16)
    shifted = pltpu.VMEM((nx + 2, ny + 2, nz, 3 * ch), BF16)
    dma = pltpu.SemaphoreType.DMA
    block = (nx, ny, nz, ch)
    out, fgrad, g1, g2 = pl.pallas_call(
        functools.partial(kernel, (ndp, npx, npy, batch * ndp)),
        out_shape=(
            jax.ShapeDtypeStruct(block, BF16),
            jax.ShapeDtypeStruct(block, BF16),
            jax.ShapeDtypeStruct((wid, rpad), F32),
            jax.ShapeDtypeStruct((wid, rpad), F32),
        ),
        in_specs=[vmem, vmem, hbm, hbm],
        out_specs=(vmem, vmem, vmem, vmem),
        scratch_shapes=[
            pltpu.VMEM((kc, ch), BF16),
            pltpu.VMEM((kc, ch), BF16),
            padded, padded, padded, padded,
            shifted, shifted, shifted,
            pltpu.VMEM((ch, cells), BF16),
            pltpu.VMEM((ch, cells), BF16),
            pltpu.VMEM((nx, ny * nz, ch), F32),
            pltpu.VMEM((2, kc, half), F32),
            pltpu.VMEM((2, kc, half), BF16),
            pltpu.VMEM((2, kc, half), BF16),
            pltpu.VMEM((2, ndp - 1, rows, half), BF16),
            pltpu.VMEM((rpad, half), F32),
            pltpu.VMEM((2, half, rpad), BF16),
            pltpu.VMEM((2, npx, wid, rpad), BF16),
            dma((2,)),
            dma((4, 8)), dma((4, 8)),
            dma((2, 9)), dma((2, 9)),
            dma((2, ndp - 1)), dma((2, ndp - 1)),
            dma((2, half // wid)), dma((2, npx)),
        ],
        compiler_params=pltpu.CompilerParams(
            collective_id=0, has_side_effects=True, vmem_limit_bytes=64000000
        ),
        name="closure",
    )(fields.reshape(block), cotangent.reshape(block), first_weight, second_weight)
    return (
        out.reshape(fields.shape),
        fgrad.reshape(fields.shape),
        g1[:, :rows].T,
        g2[:, :rows].T,
    )


def solution(mesh):
    sizes = tuple(mesh.shape[name] for name in ("dp", "px", "py"))
    placed = (P("dp", "px", "py", None, None), P("dp", "px", "py", None, None), P(), P())
    return jax.shard_map(
        functools.partial(body, sizes),
        mesh=mesh,
        in_specs=placed,
        out_specs=(
            P("dp", "px", "py", None, None),
            P("dp", "px", "py", None, None),
            P("dp", ("px", "py")),
            P("dp", ("px", "py")),
        ),
        check_vma=False,
    )
```

time: 320 us -> 83.8 us (0.26)
  the two profiles are of different devices: /device:TPU:0 before, /device:TPU:9 now
where the time goes in v1:
time: 83.8 us; the launch traced here: 83.6 us
  Pallas kernels  77.4 us (92%)
  local copies, waits for them, and re-layouts  5.58 us (7%)
    pallas_call x1, Pallas kernels, body(): pl.pallas_call(functools.partial(kernel, (ndp, npx, npy, batch * ndp)), o...  77.4 us
    unnamed x2, local copies, waits for them, and re-layouts  3.73 us
    transpose x1, local copies, waits for them, and re-layouts, body(): g2[:, :rows]  1.84 us

profile of v1, /device:TPU:9, one launch (start us, length us, event | category | flops | bytes accessed | tf_op | source)
XLA Modules:
  0.0 83.6 jit_solution(2899593398104937967)
XLA Ops:
  0.6 77.4 %closure.1 = (bf16[4,8,32,256]{3,2,1,0:T(8,128)(2,1)}, bf16[4,8,32,256]{3,2,1,0:T(8,128)(2,1)}, f32[32,1792]{1,0:T(8,128)}, f32[32,1792]{1,0:T(8,128)}) custom-call(bf16[4,8,32,256]{3,2,1,0:T(8,128)(2,1)} %bitcast.8, bf16[4,8,32,256]{3,2,1,0:T(8,128)(2,1)} %bitcast.9, bf16[6912,256]{1,0:T(8,128)(2,1)} %w1_hbm.1, bf16[6912,256]{1,0:T(8,128)(2,1)} %w2_hbm.1), custom_call_target="tpu_custom_call" | custom-call | tf_op jit(solution)/shard_map/closure/pallas_call | solution.py:328
  78.0 1.8 %slice_bitcast_fusion = (f32[1728,32]{0,1:T(8,128)}, f32[1728,32]{0,1:T(8,128)}) fusion(f32[32,1792]{1,0:T(8,128)} %get-tuple-element.11, f32[32,1792]{1,0:T(8,128)} %get-tuple-element.10), kind=kLoop, calls=%fused_computation | loop fusion | bytes 884736 | tf_op jit(solution)/shard_map/transpose | solution.py:368
  79.8 1.9 %copy.10 = bf16[1,4,8,32,256]{4,3,2,1,0:T(8,128)(2,1)} copy(bf16[1,4,8,32,256]{4,3,2,1,0:T(8,128)(2,1)} %bitcast.11) | data formatting | bytes 1048576
  81.7 1.9 %copy.11 = bf16[1,4,8,32,256]{4,3,2,1,0:T(8,128)(2,1)} copy(bf16[1,4,8,32,256]{4,3,2,1,0:T(8,128)(2,1)} %bitcast.10) | data formatting | bytes 1048576

commit v2 on v1

--- a/solution.py
+++ b/solution.py
@@ -16,6 +16,24 @@
 
 def gelu_parts(v):
     return jnp.tanh(GELU_C * (v + GELU_A * (v * v * v)))
+
+
+def dp_slots(ndp):
+    db = 2 if ndp % 2 == 0 else 1
+    da = ndp // db
+    first = [(0, 0, hop, item) for hop in range(1, db) for item in [*range(1, da), 0]]
+    other = [(0, 1, hop, item) for hop in range(1, da) for item in [*range(1, db), 0]]
+    slots = [s for pair in zip(first, other) for s in pair]
+    slots += first[len(other) :] + other[len(first) :]
+    slots += [(1, 0, hop, 0) for hop in range(1, da)] + [(1, 1, hop, 0) for hop in range(1, db)]
+    return (da, db), slots
+
+
+def results(rows, out_in, fgrad_in, g1_in, g2_in, out_ref, fgrad_ref, g1_ref, g2_ref):
+    out_ref[...] = out_in[...]
+    fgrad_ref[...] = fgrad_in[...]
+    g1_ref[...] = g1_in[:, :rows]
+    g2_ref[...] = g2_in[:, :rows]
 
 
 def kernel(
@@ -27,6 +45,7 @@
     sem_w, halo_send, halo_recv, a_send, a_recv, b_send, b_recv, z_send, z_recv,
 ):
     ndp, npx, npy, rollouts = sizes
+    factors, b_slots = dp_slots(ndp)
     nx, ny, nz, ch = fields.shape
     cells = nx * ny * nz
     half = ch // npy
@@ -114,8 +133,8 @@
 
     tile = ny * nz
 
-    def conv(shifted, weight, flipped, finish):
-        @pl.loop(0, nx)
+    def conv(shifted, weight, flipped, finish, low=0, high=nx):
+        @pl.loop(low, high)
         def _(i):
             total = None
             for a in range(3):
@@ -168,13 +187,31 @@
                 send_a[which, here] = jnp.where(y == 0, high, low).astype(BF16)
             a_copy(which, step).start()
 
-    def b_copy(which, hop):
-        peer = lax.rem(d + hop, ndp)
-        return pltpu.make_async_remote_copy(
-            src_ref=send_a.at[which, pl.ds(pl.multiple_of(peer * rows, 16), rows)],
-            dst_ref=recv_b.at[which, hop - 1],
-            send_sem=b_send.at[which, hop - 1],
-            recv_sem=b_recv.at[which, hop - 1],
+    da, db = factors
+    part_rows = rows // 2
+    ia, ib = d // db, lax.rem(d, db)
+
+    def piece(a, b, side):
+        first = (a * db + b) * rows + side * part_rows
+        return pl.ds(pl.multiple_of(first, 16), part_rows)
+
+    def ring(index, hop, count):
+        return lax.rem(index + hop, count)
+
+    def b_copy(which, phase, side, hop, item):
+        along_b = (side == 0) == (phase == 0)
+        if along_b:
+            a, b = (ring(ia, item, da) if phase == 0 else ia), ring(ib, hop, db)
+            peer = ia * db + b
+        else:
+            a, b = ring(ia, hop, da), (ring(ib, item, db) if phase == 0 else ib)
+            peer = a * db + ib
+        slot = b_slots.index((phase, side, hop, item))
+        return piece(a, b, side), pltpu.make_async_remote_copy(
+            src_ref=send_a.at[which, piece(a, b, side)],
+            dst_ref=recv_b.at[which, slot],
+            send_sem=b_send.at[which, slot],
+            recv_sem=b_recv.at[which, slot],
             device_id=(peer, x, y),
             device_id_type=MESH,
         )
@@ -184,15 +221,31 @@
         def _(step):
             a_copy(which, step).wait()
 
-        for hop in [*range(1, ndp), 0]:
-            peer = lax.rem(d + hop, ndp)
-            part = pl.ds(pl.multiple_of(peer * rows, 16), rows)
-            total = own[which, part] + recv_a[which, part].astype(F32)
-            if hop:
-                send_a[which, part] = total.astype(BF16)
-                b_copy(which, hop).start()
-            else:
-                own[which, part] = total
+        for slot in [s for s in b_slots if s[0] == 0]:
+            part, copy = b_copy(which, *slot)
+            send_a[which, part] = (own[which, part] + recv_a[which, part].astype(F32)).astype(BF16)
+            copy.start()
+        for side, count in ((0, da), (1, db)):
+            for item in range(count):
+                a, b = (ring(ia, item, da), ib) if side == 0 else (ia, ring(ib, item, db))
+                part = piece(a, b, side)
+                own[which, part] = own[which, part] + recv_a[which, part].astype(F32)
+
+    def rows_next(which):
+        for side, count, hops in ((0, da, db), (1, db, da)):
+            for item in [*range(1, count), 0]:
+                a, b = (ring(ia, item, da), ib) if side == 0 else (ia, ring(ib, item, db))
+                part = piece(a, b, side)
+                total = own[which, part]
+                for hop in range(1, hops):
+                    slot = (0, side, hop, item)
+                    b_copy(which, *slot)[1].wait()
+                    total = total + recv_b[which, b_slots.index(slot)].astype(F32)
+                if item:
+                    send_a[which, part] = total.astype(BF16)
+                    b_copy(which, 1, side, item, 0)[1].start()
+                else:
+                    own[which, part] = total
 
     def z_ids(j):
         owner = y * nj + j
@@ -210,13 +263,13 @@
         )
 
     def columns_start(which):
-        for hop in range(1, ndp):
-            b_copy(which, hop).wait()
-        part = pl.ds(pl.multiple_of(d * rows, 16), rows)
-        total = own[which, part]
-        for hop in range(1, ndp):
-            total = total + recv_b[which, hop - 1].astype(F32)
-        tot[0:rows] = total
+        for side, hops in ((0, da), (1, db)):
+            total = own[which, piece(ia, ib, side)]
+            for hop in range(1, hops):
+                slot = (1, side, hop, 0)
+                b_copy(which, *slot)[1].wait()
+                total = total + recv_b[which, b_slots.index(slot)].astype(F32)
+            tot[side * part_rows : (side + 1) * part_rows] = total
         if rpad > rows:
             tot[rows:rpad] = jnp.zeros((rpad - rows, half), F32)
         send_z[which] = tot[...].T.astype(BF16)
@@ -292,11 +345,13 @@
             (fields[i].reshape(tile, ch).astype(F32) + total).astype(BF16).reshape(ny, nz, ch)
         )
 
-    conv(z_a, w2, False, out_finish)
+    conv(z_a, w2, False, out_finish, 0, nx // 2)
     halo_wait(3, p_g, 1, p_g)
     build(p_g, z_c)
     weight_grad(0, lhs_f, z_c)
+    rows_next(1)
     rows_start(0)
+    conv(z_a, w2, False, out_finish, nx // 2, nx)
     columns_start(1)
 
     def field_finish(i, total):
@@ -304,7 +359,9 @@
             (cot[i].reshape(tile, ch).astype(F32) + total).astype(BF16).reshape(ny, nz, ch)
         )
 
-    conv(z_c, w1, True, field_finish)
+    conv(z_c, w1, True, field_finish, 0, nx // 2)
+    rows_next(0)
+    conv(z_c, w1, True, field_finish, nx // 2, nx)
     finish_grad(1, g2_ref)
     columns_start(0)
     finish_grad(0, g1_ref)
@@ -315,6 +372,7 @@
     batch, nx, ny, nz, ch = fields.shape
     kc = first_weight.shape[0]
     half = ch // npy
+    slots = dp_slots(ndp)[1]
     rows = kc // ndp
     rpad = -(-rows // 128) * 128
     wid = ch // (npx * npy)
@@ -346,14 +404,14 @@
             pltpu.VMEM((2, kc, half), F32),
             pltpu.VMEM((2, kc, half), BF16),
             pltpu.VMEM((2, kc, half), BF16),
-            pltpu.VMEM((2, ndp - 1, rows, half), BF16),
+            pltpu.VMEM((2, len(slots), rows // 2, half), BF16),
             pltpu.VMEM((rpad, half), F32),
             pltpu.VMEM((2, half, rpad), BF16),
             pltpu.VMEM((2, npx, wid, rpad), BF16),
             dma((2,)),
             dma((4, 8)), dma((4, 8)),
             dma((2, 9)), dma((2, 9)),
-            dma((2, ndp - 1)), dma((2, ndp - 1)),
+            dma((2, len(slots))), dma((2, len(slots))),
             dma((2, half // wid)), dma((2, npx)),
         ],
         compiler_params=pltpu.CompilerParams(
@@ -361,11 +419,23 @@
         ),
         name="closure",
     )(fields.reshape(block), cotangent.reshape(block), first_weight, second_weight)
+    out, fgrad, g1, g2 = pl.pallas_call(
+        functools.partial(results, rows),
+        out_shape=(
+            jax.ShapeDtypeStruct(block, BF16),
+            jax.ShapeDtypeStruct(block, BF16),
+            jax.ShapeDtypeStruct((wid, rows), F32),
+            jax.ShapeDtypeStruct((wid, rows), F32),
+        ),
+        in_specs=[vmem] * 4,
+        out_specs=(vmem,) * 4,
+        name="results",
+    )(out, fgrad, g1, g2)
     return (
         out.reshape(fields.shape),
         fgrad.reshape(fields.shape),
-        g1[:, :rows].T,
-        g2[:, :rows].T,
+        g1.T,
+        g2.T,
     )
 
 

time: 83.8 us -> 79.8 us (0.952)
  local copies, waits for them, and re-layouts: 5.58 us -> 0 us
  Pallas kernels: 77.4 us -> 78.9 us
    unnamed x2 -> x0, local copies, waits for them, and re-layouts: 3.73 us -> none
    pallas_call x0 -> x1, Pallas kernels: none -> 2.47 us  [body(): pl.pallas_call(functools.partial(results, rows), out_shape=(jax.ShapeDtyp...]
    transpose x1 -> x0, local copies, waits for them, and re-layouts: 1.84 us -> none  [body(): g2[:, :rows]]
    pallas_call x1, Pallas kernels: 77.4 us -> 76.5 us  [body(): pl.pallas_call(functools.partial(kernel, (ndp, npx, npy, batch * ndp)), o...]
where the time goes in v2:
time: 79.8 us; the launch traced here: 79.6 us
  Pallas kernels  78.9 us (99%)
    pallas_call x1, Pallas kernels, body(): pl.pallas_call(functools.partial(kernel, (ndp, npx, npy, batch * ndp)), o...  76.5 us
    pallas_call x1, Pallas kernels, body(): pl.pallas_call(functools.partial(results, rows), out_shape=(jax.ShapeDtyp...  2.47 us

profile of v2, /device:TPU:9, one launch (start us, length us, event | category | flops | bytes accessed | tf_op | source)
XLA Modules:
  0.0 79.6 jit_solution(1592113498803125592)
XLA Ops:
  0.6 76.5 %closure.1 = (bf16[4,8,32,256]{3,2,1,0:T(8,128)(2,1)}, bf16[4,8,32,256]{3,2,1,0:T(8,128)(2,1)}, f32[32,1792]{1,0:T(8,128)}, f32[32,1792]{1,0:T(8,128)}) custom-call(bf16[4,8,32,256]{3,2,1,0:T(8,128)(2,1)} %bitcast.6, bf16[4,8,32,256]{3,2,1,0:T(8,128)(2,1)} %bitcast.7, bf16[6912,256]{1,0:T(8,128)(2,1)} %w1_hbm.1, bf16[6912,256]{1,0:T(8,128)(2,1)} %w2_hbm.1), custom_call_target="tpu_custom_call" | custom-call | tf_op jit(solution)/shard_map/closure/pallas_call | solution.py:386
  77.1 2.5 %results.1 = (bf16[4,8,32,256]{3,2,1,0:T(8,128)(2,1)}, bf16[4,8,32,256]{3,2,1,0:T(8,128)(2,1)}, f32[32,1728]{1,0:T(8,128)}, f32[32,1728]{1,0:T(8,128)}) custom-call(bf16[4,8,32,256]{3,2,1,0:T(8,128)(2,1)} %get-tuple-element.12.out_in, bf16[4,8,32,256]{3,2,1,0:T(8,128)(2,1)} %get-tuple-element.13.fgrad_in, f32[32,1792]{1,0:T(8,128)} %get-tuple-element.14.g1_in, ...), custom_call_target="tpu_custom_call" | custom-call | tf_op jit(solution)/shard_map/results/pallas_call | solution.py:422

commit v3 on v2

--- a/solution.py
+++ b/solution.py
@@ -348,11 +348,11 @@
     conv(z_a, w2, False, out_finish, 0, nx // 2)
     halo_wait(3, p_g, 1, p_g)
     build(p_g, z_c)
+    rows_next(1)
     weight_grad(0, lhs_f, z_c)
-    rows_next(1)
     rows_start(0)
+    columns_start(1)
     conv(z_a, w2, False, out_finish, nx // 2, nx)
-    columns_start(1)
 
     def field_finish(i, total):
         fgrad_ref[i] = (

time: 79.8 us -> 77.1 us (0.966)
  Pallas kernels: 78.9 us -> 76.3 us
    pallas_call x1, Pallas kernels: 76.5 us -> 73.8 us  [body(): pl.pallas_call(functools.partial(kernel, (ndp, npx, npy, batch * ndp)), o...]
where the time goes in v3:
time: 77.1 us; the launch traced here: 77 us
  Pallas kernels  76.3 us (99%)
    pallas_call x1, Pallas kernels, body(): pl.pallas_call(functools.partial(kernel, (ndp, npx, npy, batch * ndp)), o...  73.8 us
    pallas_call x1, Pallas kernels, body(): pl.pallas_call(functools.partial(results, rows), out_shape=(jax.ShapeDtyp...  2.47 us

profile of v3, /device:TPU:9, one launch (start us, length us, event | category | flops | bytes accessed | tf_op | source)
XLA Modules:
  0.0 77.0 jit_solution(14645990263090221116)
XLA Ops:
  0.6 73.8 %closure.1 = (bf16[4,8,32,256]{3,2,1,0:T(8,128)(2,1)}, bf16[4,8,32,256]{3,2,1,0:T(8,128)(2,1)}, f32[32,1792]{1,0:T(8,128)}, f32[32,1792]{1,0:T(8,128)}) custom-call(bf16[4,8,32,256]{3,2,1,0:T(8,128)(2,1)} %bitcast.6, bf16[4,8,32,256]{3,2,1,0:T(8,128)(2,1)} %bitcast.7, bf16[6912,256]{1,0:T(8,128)(2,1)} %w1_hbm.1, bf16[6912,256]{1,0:T(8,128)(2,1)} %w2_hbm.1), custom_call_target="tpu_custom_call" | custom-call | tf_op jit(solution)/shard_map/closure/pallas_call | solution.py:386
  74.5 2.5 %results.1 = (bf16[4,8,32,256]{3,2,1,0:T(8,128)(2,1)}, bf16[4,8,32,256]{3,2,1,0:T(8,128)(2,1)}, f32[32,1728]{1,0:T(8,128)}, f32[32,1728]{1,0:T(8,128)}) custom-call(bf16[4,8,32,256]{3,2,1,0:T(8,128)(2,1)} %get-tuple-element.12.out_in, bf16[4,8,32,256]{3,2,1,0:T(8,128)(2,1)} %get-tuple-element.13.fgrad_in, f32[32,1792]{1,0:T(8,128)} %get-tuple-element.14.g1_in, ...), custom_call_target="tpu_custom_call" | custom-call | tf_op jit(solution)/shard_map/results/pallas_call | solution.py:422
